TPU v7x, 32 devices: a whole 2x2x4 slice. The times are simulated.
32 devices in a mesh: expert: 8 (over y, x, core), dp: 4 (over z).
Axes of the slice: x: 2, y: 2, z: 4, core: 2. Of those that a mesh axis runs over, the one named last changes fastest.
Arguments:
- tokens: bfloat16 [4096, 2048], P(('expert', 'dp')), may hold values from -6 to 6
- cotangent: bfloat16 [4096, 2048], P(('expert', 'dp')), may hold values from -6 to 6
- router_probs: float32 [4096, 6], P(('expert', 'dp')), may hold values from 0.1 to 0.6
- routes: int32 [4096, 6], P(('expert', 'dp')), may hold values from 0 to 15, all different within a row; in each aligned block of 128 rows (0 to 127, 128 to 255, ...) at most 60 rows name the same one
- partner: int32 [8], replicated, may hold values from 0 to 7, as said below
- gate_weight: bfloat16 [16, 2048, 768], P('expert'), may hold values from -0.125 to 0.125
- up_weight: bfloat16 [16, 2048, 768], P('expert'), may hold values from -0.125 to 0.125
- down_weight: bfloat16 [16, 768, 2048], P('expert'), may hold values from -0.21875 to 0.21875
Outputs:
- output: bfloat16 [4096, 2048], P(('expert', 'dp'))
- token_grad: bfloat16 [4096, 2048], P(('expert', 'dp'))
- expert_grads: bfloat16 [768, 16, 3, 2048], P('dp', 'expert')
Inputs may be any that keep to these rules, and one draw needn't show every extreme that they name: `routes`: each token names 6 different experts. Within the 128 rows of one device no expert is named by more than 60 rows, a bound that some block reaches of them. partner[j] is j or (j + 4) mod 8, and partner[partner[j]] = j.
All inputs are finite; a program needn't handle non-finite values.
Results may differ from a plain program's by a relative error of at most 0.0095.
Values may be sent and summed in bfloat16 or wider, within the bound.
A program may use at most 192 MiB of HBM per device.

v0:
```python
import jax
import jax.numpy as jnp
from jax import lax
from jax.sharding import PartitionSpec as P


def from_partner(value, axis, distance):
    mask = 2**distance
    pairs = [(source, source ^ mask) for source in range(lax.axis_size(axis))]
    return lax.ppermute(value, axis, pairs)


def forward_rows(rows_in, gate_part, up_part):
    gate_pre = jnp.einsum("necd,edf->necf", rows_in, gate_part, preferred_element_type=jnp.float32)
    up_proj = jnp.einsum("necd,edf->necf", rows_in, up_part, preferred_element_type=jnp.float32)
    sigmoid_gate = jax.nn.sigmoid(gate_pre)
    activated = gate_pre * sigmoid_gate
    hidden = (activated * up_proj).astype(jnp.bfloat16)
    return (gate_pre, up_proj, sigmoid_gate, activated, hidden)


def backward_rows(rows_cot, gate_pre, up_proj, sigmoid_gate, activated, down_part):
    grad_hidden = jnp.einsum(
        "necd,efd->necf", rows_cot, down_part, preferred_element_type=jnp.float32
    )
    grad_gate = (
        grad_hidden * up_proj * sigmoid_gate * (1.0 + gate_pre * (1.0 - sigmoid_gate))
    ).astype(jnp.bfloat16)
    grad_up = (grad_hidden * activated).astype(jnp.bfloat16)
    return (grad_gate, grad_up)


def input_grads(grad_gate, grad_up, gate_weight, up_weight):
    summed = jnp.einsum(
        "necf,edf->necd", grad_gate, gate_weight, preferred_element_type=jnp.float32
    )
    summed = summed + jnp.einsum(
        "necf,edf->necd", grad_up, up_weight, preferred_element_type=jnp.float32
    )
    return summed.astype(jnp.bfloat16)


def local(tokens, cotangent, router_probs, routes, partner, gate_weight, up_weight, down_weight):
    tok_dev = tokens.shape[0]
    model_width = tokens.shape[1]
    top_count = routes.shape[1]
    exp_dev = gate_weight.shape[0]
    hidden_units = gate_weight.shape[2]
    owners = lax.axis_size("expert")
    slot_total = exp_dev * owners
    capacity = max(2, 5 * tok_dev * top_count // (4 * slot_total))
    assigned = tok_dev * top_count
    flat_routes = routes.reshape(-1)
    blocks = flat_routes // exp_dev
    owner_ids = jnp.arange(owners, dtype=jnp.int32)
    target = jnp.sum(jnp.where(blocks[:, None] == owner_ids[None, :], partner[None, :], 0), axis=1)
    slot_key = target * exp_dev + flat_routes % exp_dev
    onehot = (slot_key[:, None] == jnp.arange(slot_total, dtype=jnp.int32)[None, :]).astype(
        jnp.int32
    )
    slot_rank = jnp.sum((jnp.cumsum(onehot, axis=0) - 1) * onehot, axis=1)
    slot_row = slot_key * capacity + slot_rank
    source = (
        jnp.full((slot_total * capacity,), assigned, jnp.int32)
        .at[slot_row]
        .set(jnp.arange(assigned, dtype=jnp.int32))
    )
    tok_index = source // top_count
    zero_row = jnp.zeros((1, model_width), jnp.bfloat16)
    padded_tokens = jnp.concatenate([tokens, zero_row], axis=0)
    padded_cot = jnp.concatenate([cotangent, zero_row], axis=0)
    padded_probs = jnp.concatenate([router_probs.reshape(-1), jnp.zeros((1,), jnp.float32)])
    send_tokens = padded_tokens[tok_index].reshape(owners, exp_dev, capacity, model_width)
    send_cot = (padded_probs[source][:, None] * padded_cot[tok_index].astype(jnp.float32)).astype(
        jnp.bfloat16
    )
    send_cot = send_cot.reshape(owners, exp_dev, capacity, model_width)
    recv_tokens, recv_cot = (
        lax.all_to_all(send_tokens, "expert", split_axis=0, concat_axis=0, tiled=True),
        lax.all_to_all(send_cot, "expert", split_axis=0, concat_axis=0, tiled=True),
    )
    gate_pre, up_proj, sigmoid_gate, activated, hidden = forward_rows(
        recv_tokens, gate_weight, up_weight
    )
    expert_out = jnp.einsum(
        "necf,efd->necd", hidden, down_weight, preferred_element_type=jnp.float32
    ).astype(jnp.bfloat16)
    grad_gate, grad_up = backward_rows(
        recv_cot, gate_pre, up_proj, sigmoid_gate, activated, down_weight
    )
    expert_dx = input_grads(grad_gate, grad_up, gate_weight, up_weight)
    back_out, back_dx = (
        lax.all_to_all(expert_out, "expert", split_axis=0, concat_axis=0, tiled=True),
        lax.all_to_all(expert_dx, "expert", split_axis=0, concat_axis=0, tiled=True),
    )
    picked_out = back_out.reshape(slot_total * capacity, model_width)[slot_row].reshape(
        tok_dev, top_count, model_width
    )
    picked_dx = back_dx.reshape(slot_total * capacity, model_width)[slot_row].reshape(
        tok_dev, top_count, model_width
    )
    output = jnp.sum(router_probs[:, :, None] * picked_out.astype(jnp.float32), axis=1).astype(
        jnp.bfloat16
    )
    token_grad = jnp.sum(picked_dx.astype(jnp.float32), axis=1).astype(jnp.bfloat16)
    quarter = hidden_units // lax.axis_size("dp")
    offset = lax.axis_index("dp") * quarter
    gate_part = lax.dynamic_slice_in_dim(gate_weight, offset, quarter, 2)
    up_part = lax.dynamic_slice_in_dim(up_weight, offset, quarter, 2)
    down_part = lax.dynamic_slice_in_dim(down_weight, offset, quarter, 1)
    rows_in = lax.all_gather(recv_tokens, "dp", axis=0, tiled=True)
    rows_cot = lax.all_gather(recv_cot, "dp", axis=0, tiled=True)
    shards = rows_in.shape[0] // owners
    part_gate, part_up, part_sigmoid, part_active, part_hidden = forward_rows(
        rows_in, gate_part, up_part
    )
    part_dgate, part_dup = backward_rows(
        rows_cot, part_gate, part_up, part_sigmoid, part_active, down_part
    )
    split_in = rows_in.reshape(shards, owners, exp_dev, capacity, model_width)
    split_cot = rows_cot.reshape(shards, owners, exp_dev, capacity, model_width)
    split_dgate = part_dgate.reshape(shards, owners, exp_dev, capacity, quarter)
    split_dup = part_dup.reshape(shards, owners, exp_dev, capacity, quarter)
    split_hidden = part_hidden.reshape(shards, owners, exp_dev, capacity, quarter)
    stacked = jnp.stack(
        [
            jnp.einsum(
                "snecf,snecd->sfed", split_dgate, split_in, preferred_element_type=jnp.float32
            ),
            jnp.einsum(
                "snecf,snecd->sfed", split_dup, split_in, preferred_element_type=jnp.float32
            ),
            jnp.einsum(
                "snecf,snecd->sfed", split_hidden, split_cot, preferred_element_type=jnp.float32
            ),
        ],
        axis=3,
    )
    rounded = lax.optimization_barrier(stacked.astype(jnp.bfloat16))
    summed = jnp.sum(rounded.astype(jnp.float32), axis=0)
    rounded_sum = summed.astype(jnp.bfloat16)
    row_here = lax.axis_index("expert")
    partner_here = jnp.sum(jnp.where(owner_ids == row_here, partner, 0))
    swap_bit = owners.bit_length() - 2
    swapped = from_partner(rounded_sum, "expert", swap_bit)
    expert_grads = jnp.where(partner_here == row_here, rounded_sum, swapped)
    return (output, token_grad, expert_grads)


def solution(mesh):
    placed = (
        P(("expert", "dp"), None),
        P(("expert", "dp"), None),
        P(("expert", "dp"), None),
        P(("expert", "dp"), None),
        P(),
        P("expert", None, None),
        P("expert", None, None),
        P("expert", None, None),
    )
    return jax.shard_map(
        local,
        mesh=mesh,
        in_specs=placed,
        out_specs=(
            P(("expert", "dp"), None),
            P(("expert", "dp"), None),
            P("dp", "expert", None, None),
        ),
        check_vma=False,
    )
```

profile of v0, /device:TPU:1, one launch (start us, length us, event | category | flops | bytes accessed | tf_op | source)
XLA Modules:
  0.0 951.5 jit_solution(2456945851649299749)
XLA Ops:
  15.9 6.0 gather_fusion
  26.7 6.2 copy.70
  33.0 50.0 %all_to_all.20 = bf16[8,2,60,2048]{3,1,2,0:T(2,128)(2,1)S(1)} all-to-all(bf16[8,2,60,2048]{3,1,2,0:T(2,128)(2,1)S(1)} %copy.70), channel_id=1, replica_groups=mesh['expert'=8,'dp'=4] {'expert'}, dimensions={0} | all-to-all | bytes 7864320 | tf_op jit(solution)/shard_map/all_to_all | solution.py:79
  89.1 5.9 gather_fusion.3
  95.0 6.6 reshape.217
  114.8 48.8 %all_to_all.21 = bf16[8,2,60,2048]{3,1,2,0:T(2,128)(2,1)S(1)} all-to-all(bf16[8,2,60,2048]{3,1,2,0:T(2,128)(2,1)S(1)} %copy.76), channel_id=1, replica_groups=mesh['expert'=8,'dp'=4] {'expert'}, dimensions={0} | all-to-all | bytes 7864320 | tf_op jit(solution)/shard_map/all_to_all | solution.py:80
  169.4 8.1 fusion.11
  187.3 5.9 copy.73
  193.2 5.7 all-to-all-start.1
  198.9 8.4 fusion.17
  209.1 5.7 fusion.9
  214.8 160.9 %all-gather.3.cloned.1.call-done = bf16[32,2,60,2048]{3,2,0,1:T(8,128)(2,1)} async-done(((bf16[8,2,60,2048]{3,2,0,1:T(8,128)(2,1)}), bf16[32,2,60,2048]{3,2,0,1:T(8,128)(2,1)}) %all-gather.3.cloned.1.call-update) | async-done | bytes 15728656 | tf_op jit(solution)/shard_map/all_gather | solution.py:111
  375.7 10.8 %fusion.52 = f32[2,192,32,60]{1,3,2,0:T(8,128)} fusion(bf16[32,2,60,2048]{3,2,0,1:T(8,128)(2,1)} %all-gather.3.cloned.1.call-done, bf16[2,2048,768]{2,1,0:T(8,128)(2,1)} %param.14, s32[]{:T(128)S(6)} %select_n.87), kind=kOutput, calls=%fused_computation.69 | convolution fusion | flops 3019898880 | bytes 21823492 | tf_op jit(solution)/shard_map/necd,edf->necf/dot_general | solution.py:15
  386.5 276.3 %all-gather.5.cloned.1.call-done = bf16[32,2,60,2048]{3,2,0,1:T(8,128)(2,1)} async-done(((bf16[8,2,60,2048]{3,2,0,1:T(8,128)(2,1)}), bf16[32,2,60,2048]{3,2,0,1:T(8,128)(2,1)}) %all-gather.5.cloned.1.call-update) | async-done | bytes 15728656 | tf_op jit(solution)/shard_map/all_gather | solution.py:112
  662.8 12.8 %fusion.62 = f32[2,192,32,60]{1,3,2,0:T(8,128)} fusion(bf16[32,2,60,2048]{3,2,0,1:T(8,128)(2,1)} %all-gather.5.cloned.1.call-done, bf16[2,768,2048]{2,1,0:T(8,128)(2,1)} %param.15, s32[]{:T(128)S(6)} %select_n.87), kind=kOutput, calls=%fused_computation.76 | convolution fusion | flops 3019898880 | bytes 21299204 | tf_op jit(solution)/shard_map/necd,efd->necf/dot_general | solution.py:23
  675.6 13.8 %fusion.33 = (bf16[32,2,60,192]{3,2,0,1:T(8,128)(2,1)}, bf16[32,2,60,192]{3,2,0,1:T(8,128)(2,1)S(1)}, bf16[32,2,60,192]{3,2,0,1:T(8,128)(2,1)}) fusion(f32[2,192,32,60]{1,3,2,0:T(8,128)} %fusion.52, f32[2,192,32,60]{1,3,2,0:T(8,128)} %fusion.62, bf16[32,2,60,2048]{3,2,0,1:T(8,128)(2,1)} %all-gather.3.cloned.1.call-done, bf16[2,2048,768]{2,1,0:T(8,128)(2,1)} %param.13, ...), kind=kOutput, calls=%fused_computation.44 | convolution fusion | flops 3030958080 | bytes 31686660 | tf_op jit(solution)/shard_map/necd,edf->necf/dot_general | solution.py:14
  689.4 9.9 %fusion.7 = bf16[4,192,2,1,2048]{4,1,2,0,3:T(8,128)(2,1)} fusion(bf16[4,8,2,60,2048]{4,3,1,0,2:T(8,128)(2,1)} %bitcast.187, bf16[4,8,2,60,192]{4,3,1,0,2:T(8,128)(2,1)} %bitcast.198), kind=kOutput, calls=%fused_computation.20 | convolution fusion | flops 3023044608 | bytes 23494656 | tf_op jit(solution)/shard_map/snecf,snecd->sfed/dot_general | solution.py:130
  699.3 9.9 %fusion.6 = bf16[4,192,2,1,2048]{4,1,2,0,3:T(8,128)(2,1)} fusion(bf16[4,8,2,60,2048]{4,3,1,0,2:T(8,128)(2,1)} %bitcast.188, bf16[4,8,2,60,192]{4,3,1,0,2:T(8,128)(2,1)} %bitcast.197), kind=kOutput, calls=%fused_computation.19 | convolution fusion | flops 3023044608 | bytes 23494656 | tf_op jit(solution)/shard_map/snecf,snecd->sfed/dot_general | solution.py:127
  709.2 9.4 fusion.8
  718.7 16.0 %pad_maximum_fusion = bf16[4,192,2,3,2048]{4,1,2,0,3:T(8,128)(2,1)} fusion(bf16[4,192,2,1,2048]{4,1,2,0,3:T(8,128)(2,1)} %fusion.8, bf16[4,192,2,1,2048]{4,1,2,0,3:T(8,128)(2,1)} %fusion.7, bf16[4,192,2,1,2048]{4,1,2,0,3:T(8,128)(2,1)} %fusion.6), kind=kLoop, calls=%fused_computation.6 | loop fusion | flops 18874368 | bytes 37748736 | tf_op jit(solution)/shard_map/stack | solution.py:125
  734.7 14.0 %reduce_sum.68 = bf16[192,2,3,2048]{3,0,1,2:T(8,128)(2,1)} reduce(bf16[4,192,2,3,2048]{4,1,2,0,3:T(8,128)(2,1)} %pad_maximum_fusion, bf16[]{:T(256)} %constant.35.clone.1), dimensions={0}, to_apply=%region_8.9 | reduce | flops 7077888 | bytes 23592962 | tf_op jit(solution)/shard_map/reduce_sum | solution.py:140
  749.9 13.2 %fusion.27 = bf16[8,2,60,2048]{3,2,0,1:T(8,128)(2,1)} fusion(f32[2,8,60,2048]{3,2,1,0:T(8,128)} %fusion.9, bf16[2,2048,768]{2,1,0:T(8,128)(2,1)} %param.13, f32[2,8,60,768]{3,2,1,0:T(8,128)} %copy-done.14, f32[2,8,60,768]{3,2,1,0:T(8,128)S(1)} %copy-done.11, f32[2,8,60,768]{3,2,1,0:T(8,128)} %copy-done.12), kind=kOutput, calls=%fused_computation.35 | convolution fusion | flops 3031203840 | bytes 26935296 | tf_op jit(solution)/shard_map/necf,edf->necd/dot_general | solution.py:34
  763.1 8.1 copy.78
  771.2 5.8 all-to-all-start.3
  778.2 5.9 copy.74
  789.0 9.0 gather_fusion.1
  801.7 92.3 %all-to-all-done.3 = bf16[8,2,60,2048]{3,1,2,0:T(2,128)(2,1)} async-done(((bf16[8,2,60,2048]{3,1,2,0:T(2,128)(2,1)}), bf16[8,2,60,2048]{3,1,2,0:T(2,128)(2,1)}, u32[]{:S(2)}, u32[]{:S(2)}) %all-to-all-start.3) | async-done | bytes 3932192 | tf_op jit(solution)/shard_map/all_to_all | solution.py:94
  894.0 5.9 copy.79
  904.8 9.0 gather_fusion.4
  916.8 5.7 reduce_sum.66
  922.6 7.5 multiply_reduce_fusion
  935.1 9.4 copy.90
  (96 shorter events, 73.4 us)
Async XLA Ops:
  7.2 368.5 %all-gather.3.cloned.1.call-start = ((), (), s32[]{:S(2)}) async-start(), calls=%async_computation.4 | async-start | bytes 20971520 | tf_op jit(solution)/shard_map/all_gather | solution.py:111
  11.4 3.4 copy-start.6
  83.0 1.9 copy-start
  84.8 4.1 copy-start.8
  84.8 4.2 copy-start.5
  88.7 574.1 %all-gather.5.cloned.1.call-start = ((), (), s32[]{:S(2)}) async-start(), calls=%async_computation.5 | async-start | bytes 20971520 | tf_op jit(solution)/shard_map/all_gather | solution.py:112
  89.0 12.6 %copy-start.3 = (f32[128,6]{1,0:T(8,128)}, f32[128,6]{1,0:T(8,128)S(1)}, u32[]{:S(2)}) copy-start(f32[128,6]{1,0:T(8,128)S(1)} %copy.65) | copy-start | bytes 9220
  163.5 1.9 copy-start.2
  169.3 8.1 slice-start.6
  169.3 8.1 copy-start.1
  169.3 8.1 slice-start.7
  169.3 13.8 %slice-start.4 = ((s8[6291456]{0:T(1024)(128)(4,1)}), s8[4194304]{0:T(1024)(128)(4,1)S(1)}, s32[]{:S(2)}) async-start(s8[6291456]{0:T(1024)(128)(4,1)} %bitcast.192), calls=%async_computation.10 | async-start | bytes 8388608
  177.5 4.1 copy-start.10
  177.5 5.7 slice-start.5
  181.5 1.6 copy-start.12
  193.2 15.9 %slice-start.2 = ((s8[6291456]{0:T(1024)(128)(4,1)}), s8[2097152]{0:T(1024)(128)(4,1)S(1)}, s32[]{:S(2)}) async-start(s8[6291456]{0:T(1024)(128)(4,1)} %bitcast.190), calls=%async_computation.8 | async-start | bytes 4194304
  193.2 578.0 %all-to-all-start.1 = ((bf16[8,2,60,2048]{3,1,2,0:T(2,128)(2,1)}), bf16[8,2,60,2048]{3,1,2,0:T(2,128)(2,1)}, u32[]{:S(2)}, u32[]{:S(2)}) async-start(bf16[8,2,60,2048]{3,1,2,0:T(2,128)(2,1)} %copy.73), calls=%async_computation.1 | async-start | bytes 7864320 | tf_op jit(solution)/shard_map/all_to_all | solution.py:93
  198.9 10.2 %slice-start.3 = ((s8[6291456]{0:T(1024)(128)(4,1)}), s8[4194304]{0:T(1024)(128)(4,1)S(1)}, s32[]{:S(2)}) async-start(s8[6291456]{0:T(1024)(128)(4,1)} %bitcast.190), calls=%async_computation.9 | async-start | bytes 8388608
  198.9 10.2 %copy-start.13 = (f32[2,8,60,768]{3,2,1,0:T(8,128)S(1)}, f32[2,8,60,768]{3,2,1,0:T(8,128)}, u32[]{:S(2)}) copy-start(f32[2,8,60,768]{3,2,1,0:T(8,128)} %copy-done.12) | copy-start | bytes 8847364
  207.3 1.8 copy-start.14
  734.7 15.2 %copy-start.11 = (f32[2,8,60,768]{3,2,1,0:T(8,128)S(1)}, f32[2,8,60,768]{3,2,1,0:T(8,128)}, u32[]{:S(2)}) copy-start(f32[2,8,60,768]{3,2,1,0:T(8,128)} %copy-done.10) | copy-start | bytes 8847364
  748.7 181.5 %collective-permute-start = (bf16[192,2,3,2048]{3,0,1,2:T(8,128)(2,1)}, bf16[192,2,3,2048]{3,0,1,2:T(8,128)(2,1)}, u32[]{:S(2)}, u32[]{:S(2)}) collective-permute-start(bf16[192,2,3,2048]{3,0,1,2:T(8,128)(2,1)} %reduce_sum.68), channel_id=1, source_target_pairs={{0,16},{4,20},{8,24},{12,28},{16,0},{20,4},{24,8},{28,12},{1,17},{... | collective-permute-start | bytes 14155784 | tf_op jit(solution)/shard_map/ppermute | solution.py:10
  771.2 5.8 copy-start.9
  771.2 7.0 copy-start.7
  771.2 122.7 %all-to-all-start.3 = ((bf16[8,2,60,2048]{3,1,2,0:T(2,128)(2,1)}), bf16[8,2,60,2048]{3,1,2,0:T(2,128)(2,1)}, u32[]{:S(2)}, u32[]{:S(2)}) async-start(bf16[8,2,60,2048]{3,1,2,0:T(2,128)(2,1)} %copy.78), calls=%async_computation.3 | async-start | bytes 7864320 | tf_op jit(solution)/shard_map/all_to_all | solution.py:94
  916.8 5.8 copy-start.4
  916.8 13.3 %slice-start = ((s8[4718592]{0:T(1024)(128)(4,1)}), s8[524288]{0:T(1024)(128)(4,1)S(1)}, s32[]{:S(2)}) async-start(s8[4718592]{0:T(1024)(128)(4,1)} %bitcast.184), calls=%async_computation.6 | async-start | bytes 1048576
  922.6 7.6 slice-start.1
Sparse Core Ops, SparseCore 0:
  88.8 286.8 all-gather.2
  377.8 284.9 all-gather.4
where the time goes:
time: 960 us; the launch traced here: 951 us
  waiting for transfers between devices  530 us (55%)
  local copies, waits for them, and re-layouts  129 us (13%)
  matrix products  110 us (11%)
  blocking collectives  98.8 us (10%)
  other arithmetic  56 us (6%)
  between operations  15.2 us (2%)
  starting transfers between devices  12.9 us (1%)
    all_gather x1, waiting for transfers between devices, local(): rows_cot = lax.all_gather(recv_cot, 'dp', axis=0, tiled=True)  276 us
    all_gather x1, waiting for transfers between devices, local(): rows_in = lax.all_gather(recv_tokens, 'dp', axis=0, tiled=True)  161 us
    all_to_all x1, waiting for transfers between devices, local(): lax.all_to_all(expert_dx, 'expert', split_axis=0, concat_axis=0, tiled=True)  92.3 us
    all_to_all x1, blocking collectives, local(): lax.all_to_all(send_tokens, 'expert', split_axis=0, concat_axis=0, tiled=...  50 us
    all_to_all x1, blocking collectives, local(): lax.all_to_all(send_cot, 'expert', split_axis=0, concat_axis=0, tiled=True)  48.8 us
    dot_general x2, matrix products, backward_rows(): jnp.einsum('necd,efd->necf', rows_cot, down_part, preferred_element_type=...  21.2 us
  transfers between devices with their start and end apart: 5, of which 3 were waited for; matrix products, arithmetic and copies ran while one was open for 26% of the time, Pallas kernels for 0%

commit v1 on v0

--- a/solution.py
+++ b/solution.py
@@ -2,6 +2,14 @@
 import jax.numpy as jnp
 from jax import lax
 from jax.sharding import PartitionSpec as P
+
+
+def types_handle(vec, my_tile):
+    return jnp.split(
+        lax.all_gather(jnp.concatenate([vec, my_tile], axis=1), axis_name="dp", axis=0, tiled=True),
+        [vec.shape[1]],
+        axis=1,
+    )
 
 
 def from_partner(value, axis, distance):
@@ -108,8 +116,7 @@
     gate_part = lax.dynamic_slice_in_dim(gate_weight, offset, quarter, 2)
     up_part = lax.dynamic_slice_in_dim(up_weight, offset, quarter, 2)
     down_part = lax.dynamic_slice_in_dim(down_weight, offset, quarter, 1)
-    rows_in = lax.all_gather(recv_tokens, "dp", axis=0, tiled=True)
-    rows_cot = lax.all_gather(recv_cot, "dp", axis=0, tiled=True)
+    rows_in, rows_cot = types_handle(recv_tokens, recv_cot)
     shards = rows_in.shape[0] // owners
     part_gate, part_up, part_sigmoid, part_active, part_hidden = forward_rows(
         rows_in, gate_part, up_part

time: 960 us -> 1050 us (1.094)
  waiting for transfers between devices: 530 us -> 657 us
  blocking collectives: 98.8 us -> 0 us
  local copies, waits for them, and re-layouts: 129 us -> 154 us
  starting transfers between devices: 12.9 us -> 29.5 us
    all_to_all x2 -> x0, blocking collectives: 98.8 us -> none  [the longest x1 50 us: local(): lax.all_to_all(send_tokens, 'expert', split_axis=0, concat_axis=0, tiled=...]
    all_to_all x1, waiting for transfers between devices: 0.01 us -> 95.8 us  [local(): lax.all_to_all(expert_out, 'expert', split_axis=0, concat_axis=0, tiled=T...]
    all_to_all x1, waiting for transfers between devices: 92.3 us -> 0.01 us  [local(): lax.all_to_all(expert_dx, 'expert', split_axis=0, concat_axis=0, tiled=True)]
    all_gather x2 -> x1, waiting for transfers between devices: 437 us -> 501 us  [types_handle(): lax.all_gather(jnp.concatenate([vec, my_tile], axis=1), axis_name='dp', a...]
    all_to_all x0 -> x2, waiting for transfers between devices: none -> 60.3 us  [the longest x1 36.4 us: local(): lax.all_to_all(send_tokens, 'expert', split_axis=0, concat_axis=0, tiled=...]
    split x0 -> x1, local copies, waits for them, and re-layouts: none -> 23.4 us  [types_handle(): jnp.split(lax.all_gather(jnp.concatenate([vec, my_tile], axis=1), axis_na...]
    all_to_all x0 -> x2, starting transfers between devices: none -> 13.5 us  [the longest x1 7.9 us: local(): lax.all_to_all(send_tokens, 'expert', split_axis=0, concat_axis=0, tiled=...]
  transfers between devices with their start and end apart: 5 -> 6, of which waited for: 3 -> 4; matrix products, arithmetic and copies ran while one was open for 26% -> 26% of each run, Pallas kernels for 0% -> 0%
where the time goes in v1:
time: 1050 us; the launch traced here: 1040 us
  waiting for transfers between devices  657 us (63%)
  local copies, waits for them, and re-layouts  154 us (15%)
  matrix products  120 us (11%)
  other arithmetic  62.9 us (6%)
  starting transfers between devices  29.5 us (3%)
  between operations  15.4 us (1%)
    all_gather x1, waiting for transfers between devices, types_handle(): lax.all_gather(jnp.concatenate([vec, my_tile], axis=1), axis_name='dp', a...  501 us
    all_to_all x1, waiting for transfers between devices, local(): lax.all_to_all(expert_out, 'expert', split_axis=0, concat_axis=0, tiled=T...  95.8 us
    all_to_all x1, waiting for transfers between devices, local(): lax.all_to_all(send_tokens, 'expert', split_axis=0, concat_axis=0, tiled=...  36.4 us
    all_to_all x1, waiting for transfers between devices, local(): lax.all_to_all(send_cot, 'expert', split_axis=0, concat_axis=0, tiled=True)  23.8 us
    split x1, local copies, waits for them, and re-layouts, types_handle(): jnp.split(lax.all_gather(jnp.concatenate([vec, my_tile], axis=1), axis_na...  23.4 us
    dot_general x2, matrix products, forward_rows(): jnp.einsum('necd,edf->necf', rows_in, gate_part, preferred_element_type=j...  22.8 us
    dot_general x2, matrix products, backward_rows(): jnp.einsum('necd,efd->necf', rows_cot, down_part, preferred_element_type=...  22.7 us
  transfers between devices with their start and end apart: 6, of which 4 were waited for; matrix products, arithmetic and copies ran while one was open for 26% of the time, Pallas kernels for 0%

profile of v1, /device:TPU:1, one launch (start us, length us, event | category | flops | bytes accessed | tf_op | source)
XLA Modules:
  0.0 1039.0 jit_solution(12501414740318853729)
XLA Ops:
  22.3 6.0 reshape.217
  37.5 5.9 copy.76
  49.1 5.9 gather_fusion
  59.9 8.1 copy.70
  68.0 23.8 %all-to-all-done.2 = bf16[8,2,60,2048]{3,1,2,0:T(2,128)(2,1)} async-done(((bf16[8,2,60,2048]{3,1,2,0:T(2,128)(2,1)}), bf16[8,2,60,2048]{3,1,2,0:T(2,128)(2,1)}, u32[]{:S(2)}, u32[]{:S(2)}) %all-to-all-start.2) | async-done | bytes 3932192 | tf_op jit(solution)/shard_map/all_to_all | solution.py:88
  91.9 7.9 all-to-all-start
  100.2 6.0 copy.77
  106.1 36.4 %all-to-all-done = bf16[8,2,60,2048]{3,1,2,0:T(2,128)(2,1)} async-done(((bf16[8,2,60,2048]{3,1,2,0:T(2,128)(2,1)}), bf16[8,2,60,2048]{3,1,2,0:T(2,128)(2,1)}, u32[]{:S(2)}, u32[]{:S(2)}) %all-to-all-start) | async-done | bytes 3932192 | tf_op jit(solution)/shard_map/all_to_all | solution.py:87
  148.4 7.5 pad_maximum_fusion.1
  156.0 9.9 fusion.17
  165.9 9.0 fusion.15
  174.9 8.5 fusion.11
  189.1 13.5 %fusion.27 = bf16[8,2,60,2048]{3,2,0,1:T(8,128)(2,1)} fusion(f32[2,8,60,2048]{3,2,1,0:T(8,128)} %fusion.9, bf16[2,2048,768]{2,1,0:T(8,128)(2,1)} %param.13, f32[2,8,60,768]{3,2,1,0:T(8,128)} %fusion.17, f32[2,8,60,768]{3,2,1,0:T(8,128)} %fusion.11, f32[2,8,60,768]{3,2,1,0:T(8,128)S(1)} %copy-done.7), kind=kOutput, calls=%fused_computation.36 | convolution fusion | flops 3031203840 | bytes 26935296 | tf_op jit(solution)/shard_map/necf,edf->necd/dot_general | solution.py:42
  202.6 8.2 copy.78
  210.8 8.8 all-to-all-start.3
  219.6 501.2 %all-gather.2.cloned.1.call-done = bf16[32,4,60,2048]{3,2,0,1:T(8,128)(2,1)} async-done(((bf16[8,4,60,2048]{3,2,0,1:T(8,128)(2,1)}), bf16[32,4,60,2048]{3,2,0,1:T(8,128)(2,1)}) %all-gather.2.cloned.1.call-update) | async-done | bytes 31457296 | tf_op jit(solution)/shard_map/all_gather | solution.py:9
  720.7 10.6 %fusion.52 = f32[2,192,32,60]{1,3,2,0:T(8,128)} fusion(bf16[2,2048,768]{2,1,0:T(8,128)(2,1)} %param.14, s32[]{:T(128)S(6)} %select_n.87, bf16[32,4,60,2048]{3,2,0,1:T(8,128)(2,1)} %all-gather.2.cloned.1.call-done), kind=kOutput, calls=%fused_computation.70 | convolution fusion | flops 3019898880 | bytes 21823492 | tf_op jit(solution)/shard_map/necd,edf->necf/dot_general | solution.py:23
  731.3 12.8 %fusion.62 = f32[2,192,32,60]{1,3,2,0:T(8,128)} fusion(bf16[2,768,2048]{2,1,0:T(8,128)(2,1)} %param.15, s32[]{:T(128)S(6)} %select_n.87, bf16[32,4,60,2048]{3,2,0,1:T(8,128)(2,1)} %all-gather.2.cloned.1.call-done), kind=kOutput, calls=%fused_computation.77 | convolution fusion | flops 3019898880 | bytes 21299204 | tf_op jit(solution)/shard_map/necd,efd->necf/dot_general | solution.py:31
  744.1 23.4 %fusion.93 = (bf16[32,2,60,2048]{3,2,0,1:T(8,128)(2,1)}, bf16[32,2,60,2048]{3,2,0,1:T(8,128)(2,1)}) fusion(bf16[32,4,60,2048]{3,2,0,1:T(8,128)(2,1)} %all-gather.2.cloned.1.call-done), kind=kLoop, calls=%fused_computation.139 | loop fusion | bytes 62914560 | tf_op jit(solution)/shard_map/split | solution.py:8
  767.5 13.8 %fusion.33 = (bf16[32,2,60,192]{3,2,0,1:T(8,128)(2,1)}, bf16[32,2,60,192]{3,2,0,1:T(8,128)(2,1)S(1)}, bf16[32,2,60,192]{3,2,0,1:T(8,128)(2,1)}) fusion(f32[2,192,32,60]{1,3,2,0:T(8,128)} %fusion.52, f32[2,192,32,60]{1,3,2,0:T(8,128)} %fusion.62, bf16[32,4,60,2048]{3,2,0,1:T(8,128)(2,1)} %all-gather.2.cloned.1.call-done, bf16[2,2048,768]{2,1,0:T(8,128)(2,1)} %param.13, ...), kind=kOutput, calls=%fused_computation.45 | convolution fusion | flops 3030958080 | bytes 31686660 | tf_op jit(solution)/shard_map/necd,edf->necf/dot_general | solution.py:22
  781.3 10.4 fusion.6
  791.7 9.9 fusion.7
  801.6 9.2 fusion.8
  810.8 16.0 %pad_maximum_fusion = bf16[4,192,2,3,2048]{4,1,2,0,3:T(8,128)(2,1)} fusion(bf16[4,192,2,1,2048]{4,1,2,0,3:T(8,128)(2,1)} %fusion.8, bf16[4,192,2,1,2048]{4,1,2,0,3:T(8,128)(2,1)} %fusion.7, bf16[4,192,2,1,2048]{4,1,2,0,3:T(8,128)(2,1)} %fusion.6), kind=kLoop, calls=%fused_computation.6 | loop fusion | flops 18874368 | bytes 37748736 | tf_op jit(solution)/shard_map/stack | solution.py:132
  826.9 14.1 %reduce_sum.68 = bf16[192,2,3,2048]{3,0,1,2:T(8,128)(2,1)} reduce(bf16[4,192,2,3,2048]{4,1,2,0,3:T(8,128)(2,1)} %pad_maximum_fusion, bf16[]{:T(256)} %constant.35.clone.1), dimensions={0}, to_apply=%region_8.9 | reduce | flops 7077888 | bytes 23592962 | tf_op jit(solution)/shard_map/reduce_sum | solution.py:147
  842.2 7.2 convert_bitcast_fusion
  862.2 5.9 copy.79
  873.0 9.0 gather_fusion.4
  890.5 95.8 %all-to-all-done.1 = bf16[8,2,60,2048]{3,1,2,0:T(2,128)(2,1)} async-done(((bf16[8,2,60,2048]{3,1,2,0:T(2,128)(2,1)}), bf16[8,2,60,2048]{3,1,2,0:T(2,128)(2,1)}, u32[]{:S(2)}, u32[]{:S(2)}) %all-to-all-start.1) | async-done | bytes 3932192 | tf_op jit(solution)/shard_map/all_to_all | solution.py:101
  997.1 9.2 gather_fusion.1
  1010.0 7.4 multiply_reduce_fusion
  1022.3 9.4 copy.90
  (77 shorter events, 92.8 us)
Async XLA Ops:
  11.3 0.6 copy-start.3
  22.3 6.0 copy-start.5
  28.4 0.6 copy-start
  43.4 5.6 copy-start.2
  43.4 48.4 %all-to-all-start.2 = ((bf16[8,2,60,2048]{3,1,2,0:T(2,128)(2,1)}), bf16[8,2,60,2048]{3,1,2,0:T(2,128)(2,1)}, u32[]{:S(2)}, u32[]{:S(2)}) async-start(bf16[8,2,60,2048]{3,1,2,0:T(2,128)(2,1)} %copy.76), calls=%async_computation.2 | async-start | bytes 7864320 | tf_op jit(solution)/shard_map/all_to_all | solution.py:88
  91.9 50.7 %all-to-all-start = ((bf16[8,2,60,2048]{3,1,2,0:T(2,128)(2,1)}), bf16[8,2,60,2048]{3,1,2,0:T(2,128)(2,1)}, u32[]{:S(2)}, u32[]{:S(2)}) async-start(bf16[8,2,60,2048]{3,1,2,0:T(2,128)(2,1)} %copy.70), calls=%async_computation | async-start | bytes 7864320 | tf_op jit(solution)/shard_map/all_to_all | solution.py:87
  99.8 621.0 %all-gather.2.cloned.1.call-start = ((), (), s32[]{:S(2)}) async-start(), calls=%async_computation.4 | async-start | bytes 41943040 | tf_op jit(solution)/shard_map/all_gather | solution.py:9
  155.9 10.0 slice-start.2
  155.9 10.0 slice-start.3
  156.0 19.0 %slice-start = ((s8[6291456]{0:T(1024)(128)(4,1)}), s8[4194304]{0:T(1024)(128)(4,1)S(1)}, s32[]{:S(2)}) async-start(s8[6291456]{0:T(1024)(128)(4,1)} %bitcast.185), calls=%async_computation.5 | async-start | bytes 8388608
  165.9 9.0 slice-start.1
  174.9 8.6 copy-start.7
  174.9 8.6 copy-start.9
  210.8 644.5 %all-to-all-start.3 = ((bf16[8,2,60,2048]{3,1,2,0:T(2,128)(2,1)}), bf16[8,2,60,2048]{3,1,2,0:T(2,128)(2,1)}, u32[]{:S(2)}, u32[]{:S(2)}) async-start(bf16[8,2,60,2048]{3,1,2,0:T(2,128)(2,1)} %copy.78), calls=%async_computation.3 | async-start | bytes 7864320 | tf_op jit(solution)/shard_map/all_to_all | solution.py:102
  826.9 15.3 %copy-start.8 = (f32[2,8,60,768]{3,2,1,0:T(8,128)S(1)}, f32[2,8,60,768]{3,2,1,0:T(8,128)}, u32[]{:S(2)}) copy-start(f32[2,8,60,768]{3,2,1,0:T(8,128)} %fusion.15) | copy-start | bytes 8847364
  841.0 176.4 %collective-permute-start = (bf16[192,2,3,2048]{3,0,1,2:T(8,128)(2,1)}, bf16[192,2,3,2048]{3,0,1,2:T(8,128)(2,1)}, u32[]{:S(2)}, u32[]{:S(2)}) collective-permute-start(bf16[192,2,3,2048]{3,0,1,2:T(8,128)(2,1)} %reduce_sum.68), channel_id=1, source_target_pairs={{0,16},{4,20},{8,24},{12,28},{16,0},{20,4},{24,8},{28,12},{1,17},{... | collective-permute-start | bytes 14155784 | tf_op jit(solution)/shard_map/ppermute | solution.py:18
  855.3 5.6 copy-start.6
  855.3 6.9 copy-start.4
  855.3 131.0 %all-to-all-start.1 = ((bf16[8,2,60,2048]{3,1,2,0:T(2,128)(2,1)}), bf16[8,2,60,2048]{3,1,2,0:T(2,128)(2,1)}, u32[]{:S(2)}, u32[]{:S(2)}) async-start(bf16[8,2,60,2048]{3,1,2,0:T(2,128)(2,1)} %copy.73), calls=%async_computation.1 | async-start | bytes 7864320 | tf_op jit(solution)/shard_map/all_to_all | solution.py:101
  1006.3 3.7 copy-start.1
Sparse Core Ops, SparseCore 0:
  156.1 564.6 all-gather.1
